TPU v7x, 32 devices: a whole 2x2x4 slice. The times are simulated.
32 devices in a mesh: groups: 2 (over y), ctx: 4 (over z), dp: 2 (over x), rep: 2 (over core).
Axes of the slice: x: 2, y: 2, z: 4, core: 2. Of those that a mesh axis runs over, the one named last changes fastest.
Arguments:
- features: float32 [8, 4096, 128], P(('groups', 'dp', 'rep'), 'ctx'), parts along dimension 0, may hold values from -6 to 6
- cotangent: float32 [8, 4096, 128], P(('groups', 'dp', 'rep'), 'ctx'), parts along dimension 0, may hold values from -6 to 6
- norm_gains: float32 [2, 128], replicated, may hold values from 0.5 to 1.5
- depth_taps: float32 [2, 7, 128], replicated, may hold values from -2 to 2
- w_in: float32 [2, 128, 256], replicated, may hold values from -0.5 to 0.5
- w_out: float32 [2, 256, 128], replicated, may hold values from -0.375 to 0.375
Outputs:
- grad_features: float32 [8, 4096, 128], P(('groups', 'dp', 'rep'), 'ctx'), parts along dimension 0
- grad_gains: float32 [4, 128], P('groups'), parts along dimension 0
- grad_taps: float32 [4, 7, 128], P('groups'), parts along dimension 0
- grad_w_in: float32 [4, 128, 256], P('groups'), parts along dimension 0
- grad_w_out: float32 [4, 256, 128], P('groups'), parts along dimension 0
There are 2 independent parts, one for each index of `groups`. A program takes and returns all parts, laid end to end along the dimension named above; an argument that names none is the same for every part. Nothing has to cross between parts.
All inputs are finite; a program needn't handle non-finite values.
Results may differ from a plain program's by a relative error of at most 0.0001.
Values sent between devices are 32-bit elements; how exact they have to be, the bound alone decides.
A program may use at most 64 MiB of HBM per device.

v0:
```python
import jax
import jax.numpy as jnp
from jax import lax
from jax.sharding import PartitionSpec as P

FIRST_SPACING = 16
SECOND_SPACING = 256
BLOCKS = 2
STABILIZER = 1e-06


def with_halo(block, sides, width):
    for axis, dim in sides:
        count = lax.axis_size(axis)
        forward = [(i, i + 1) for i in range(count - 1)]
        backward = [(target, source) for source, target in forward]
        low = lax.ppermute(
            lax.slice_in_dim(block, block.shape[dim] - width, None, axis=dim), axis, forward
        )
        high = lax.ppermute(lax.slice_in_dim(block, 0, width, axis=dim), axis, backward)
        block = jnp.concatenate([low, block, high], axis=dim)
    return block


def rms_norm(stream, gain_vec):
    scale = lax.rsqrt(jnp.mean(stream * stream, axis=-1, keepdims=True) + STABILIZER)
    return stream * scale * gain_vec


def depth_sweep(padded, tap_weights, dilation, row_count):
    total = tap_weights[0] * padded[:, 0:row_count]
    for offset in range(1, tap_weights.shape[0]):
        total = (
            total
            + tap_weights[offset] * padded[:, offset * dilation : offset * dilation + row_count]
        )
    return total


def forward_block(stream, gain_vec, tap_weights, w_in, w_out, dilation):
    rim_width = tap_weights.shape[0] // 2 * dilation
    normed = rms_norm(stream, gain_vec)
    padded = with_halo(normed, (("ctx", 1),), rim_width)
    conv_out = depth_sweep(padded, tap_weights, dilation, stream.shape[1])
    pre_act = jnp.einsum("brc,ch->brh", conv_out, w_in, precision=lax.Precision.HIGHEST)
    act_out = jax.nn.silu(pre_act)
    result = stream + jnp.einsum("brh,hc->brc", act_out, w_out, precision=lax.Precision.HIGHEST)
    return (result, (stream, padded, conv_out, pre_act, act_out))


def backward_block(grad_out, saved_state, gain_vec, tap_weights, w_in, w_out, dilation):
    stream, padded, conv_out, pre_act, act_out = saved_state
    row_count = stream.shape[1]
    tap_count = tap_weights.shape[0]
    rim_width = tap_count // 2 * dilation
    grad_wout = jnp.einsum("brh,brc->hc", act_out, grad_out, precision=lax.Precision.HIGHEST)
    activation_gradient = jnp.einsum(
        "brc,hc->brh", grad_out, w_out, precision=lax.Precision.HIGHEST
    )
    sigmoid_val = jax.nn.sigmoid(pre_act)
    grad_pre = activation_gradient * (sigmoid_val * (1.0 + pre_act * (1.0 - sigmoid_val)))
    grad_win = jnp.einsum("brc,brh->ch", conv_out, grad_pre, precision=lax.Precision.HIGHEST)
    grad_conv = jnp.einsum("brh,ch->brc", grad_pre, w_in, precision=lax.Precision.HIGHEST)
    grad_tapw = jnp.stack(
        [
            jnp.sum(
                grad_conv * padded[:, offset * dilation : offset * dilation + row_count],
                axis=(0, 1),
            )
            for offset in range(tap_count)
        ]
    )
    grad_rims = with_halo(grad_conv, (("ctx", 1),), rim_width)
    grad_norm = depth_sweep(grad_rims, tap_weights[::-1], dilation, row_count)
    unused_out, norm_back = jax.vjp(rms_norm, stream, gain_vec)
    grad_stream, grad_gain = norm_back(grad_norm)
    return (grad_stream + grad_out, (grad_gain, grad_tapw, grad_win, grad_wout))


def local(features, cotangent, norm_gains, depth_taps, w_in, w_out):
    spacing_list = (FIRST_SPACING, SECOND_SPACING)
    stream = features
    saved_list = []
    for block_index in range(BLOCKS):
        stream, saved_state = forward_block(
            stream,
            norm_gains[block_index],
            depth_taps[block_index],
            w_in[block_index],
            w_out[block_index],
            spacing_list[block_index],
        )
        saved_list.append(saved_state)
    grad_flow = cotangent
    block_grads = [None] * BLOCKS
    for block_index in reversed(range(BLOCKS)):
        grad_flow, local_grads = backward_block(
            grad_flow,
            saved_list[block_index],
            norm_gains[block_index],
            depth_taps[block_index],
            w_in[block_index],
            w_out[block_index],
            spacing_list[block_index],
        )
        block_grads[block_index] = local_grads
    gain_total = jnp.stack([block_grads[index_b][0] for index_b in range(BLOCKS)])
    taps_total = jnp.stack([block_grads[index_b][1] for index_b in range(BLOCKS)])
    input_weight_sum = jnp.stack([block_grads[index_b][2] for index_b in range(BLOCKS)])
    wout_total = jnp.stack([block_grads[index_b][3] for index_b in range(BLOCKS)])
    gain_total, taps_total, input_weight_sum, wout_total = lax.psum(
        (gain_total, taps_total, input_weight_sum, wout_total), ("ctx", "dp", "rep")
    )
    return (grad_flow, gain_total, taps_total, input_weight_sum, wout_total)


def solution(mesh):
    return jax.shard_map(
        local,
        mesh=mesh,
        in_specs=(
            P(("groups", "dp", "rep"), "ctx", None),
            P(("groups", "dp", "rep"), "ctx", None),
            P(),
            P(),
            P(),
            P(),
        ),
        out_specs=(
            P(("groups", "dp", "rep"), "ctx", None),
            P("groups", None),
            P("groups", None, None),
            P("groups", None, None),
            P("groups", None, None),
        ),
        check_vma=False,
    )
```

profile of v0, /device:TPU:1, one launch (start us, length us, event | category | flops | bytes accessed | tf_op | source)
XLA Modules:
  0.0 171.0 jit_solution(2257633979996218653)
XLA Ops:
  7.2 0.0 copy-start
  7.2 0.0 all-reduce.4.cloned.1.call-start
  7.2 0.8 slice_bitcast_fusion.5
  8.0 1.2 multiply_reduce_fusion.19
  9.3 0.2 multiply_multiply_fusion.1
  9.5 0.0 copy-start.20
  9.5 1.3 collective-permute-start.1
  10.8 4.7 %collective-permute-start = (f32[1,48,128]{2,1,0:T(8,128)S(1)}, f32[1,48,128]{2,1,0:T(8,128)S(1)}, u32[]{:S(2)}, u32[]{:S(2)}) collective-permute-start(f32[1,48,128]{2,1,0:T(8,128)S(1)} %get-tuple-element.47), channel_id=1, source_target_pairs={{0,4},{4,8},{8,12},{1,5},{5,9},{9,13},{2,6},{6,10},{10,14},{3,7},{... | collective-permute-start | bytes 73736 | tf_op jit(solution)/shard_map/ppermute | solution.py:17
  15.6 0.0 collective-permute-done.1
  15.7 0.0 copy-start.11
  15.7 0.7 collective-permute-done
  16.5 0.0 copy-start.9
  16.5 0.2 multiply_add_fusion.1
  16.7 0.3 copy-done.13
  17.0 0.4 copy-done.9
  17.4 1.0 fusion.51
  18.4 1.2 multiply_reduce_fusion.18
  19.6 0.2 multiply_multiply_fusion
  19.8 0.1 fusion.83
  19.9 1.3 collective-permute-start.3
  21.2 4.3 %collective-permute-start.2 = (f32[1,768,128]{2,1,0:T(8,128)S(1)}, f32[1,768,128]{2,1,0:T(8,128)S(1)}, u32[]{:S(2)}, u32[]{:S(2)}) collective-permute-start(f32[1,768,128]{2,1,0:T(8,128)S(1)} %get-tuple-element.45), channel_id=1, source_target_pairs={{0,4},{4,8},{8,12},{1,5},{5,9},{9,13},{2,6},{6,10},{10,14},{3,7},{... | collective-permute-start | bytes 1179656 | tf_op jit(solution)/shard_map/ppermute | solution.py:17
  25.5 5.6 %collective-permute-done.3 = f32[1,768,128]{2,1,0:T(8,128)S(1)} collective-permute-done((f32[1,768,128]{2,1,0:T(8,128)S(1)}, f32[1,768,128]{2,1,0:T(8,128)S(1)}, u32[]{:S(2)}, u32[]{:S(2)}) %collective-permute-start.3) | collective-permute-done | bytes 393248 | tf_op jit(solution)/shard_map/ppermute | solution.py:20
  31.1 0.9 collective-permute-done.2
  32.1 0.2 multiply_add_fusion
  32.3 0.0 copy-start.6
  32.3 1.0 fusion.48
  33.3 1.0 copy-done.3
  34.3 1.1 convolution_multiply_fusion.1
  35.4 1.7 multiply_reduce_fusion
  37.1 0.9 fusion.82
  38.1 4.1 %collective-permute-start.4 = (f32[1,768,128]{2,1,0:T(8,128)}, f32[1,768,128]{2,1,0:T(8,128)S(1)}, u32[]{:S(2)}, u32[]{:S(2)}) collective-permute-start(f32[1,768,128]{2,1,0:T(8,128)} %get-tuple-element.42), channel_id=1, source_target_pairs={{0,4},{4,8},{8,12},{1,5},{5,9},{9,13},{2,6},{6,10},{10,14},{3,7},{... | collective-permute-start | bytes 1179656 | tf_op jit(solution)/shard_map/ppermute | solution.py:17
  42.2 1.5 collective-permute-start.5
  43.7 1.3 stack.103
  45.0 2.4 %convolution_bitcast_fusion.3 = f32[1,128,256]{2,1,0:T(8,128)S(1)} fusion(f32[1024,256]{1,0:T(8,128)} %copy-done.5, f32[1,1024,128]{2,1,0:T(8,128)S(1)} %multiply_add_fusion), kind=kOutput, calls=%fused_computation.6 | convolution fusion | flops 402653184 | bytes 1703936 | tf_op jit(solution)/shard_map/brc,brh->ch/dot_general | solution.py:62
  47.4 0.0 copy-start.19
  47.4 1.9 %convolution_bitcast_fusion.1 = f32[1,256,128]{2,1,0:T(8,128)S(1)} fusion(f32[1024,256]{1,0:T(8,128)S(1)} %copy-done.4, f32[1,1024,128]{2,1,0:T(8,128)S(1)} %copy-done.7), kind=kOutput, calls=%fused_computation.4 | convolution fusion | flops 403701760 | bytes 1703936 | tf_op jit(solution)/shard_map/brh,brc->hc/dot_general | solution.py:56
  49.3 0.0 collective-permute-done.4
  49.4 2.6 %collective-permute-done.5 = f32[1,768,128]{2,1,0:T(8,128)} collective-permute-done((f32[1,768,128]{2,1,0:T(8,128)}, f32[1,768,128]{2,1,0:T(8,128)}, u32[]{:S(2)}, u32[]{:S(2)}) %collective-permute-start.5) | collective-permute-done | bytes 393248 | tf_op jit(solution)/shard_map/ppermute | solution.py:20
  52.0 1.7 multiply_reduce_fusion.14
  53.7 0.3 fusion.21
  54.1 0.9 copy-done.2
  54.9 1.9 %convolution_bitcast_fusion.2 = f32[1,256,128]{2,1,0:T(8,128)S(1)} fusion(f32[1,1024,128]{2,1,0:T(8,128)S(1)} %fusion.21, f32[1024,256]{1,0:T(8,128)S(1)} %copy-done.2), kind=kOutput, calls=%fused_computation.5 | convolution fusion | flops 403701760 | bytes 1703936 | tf_op jit(solution)/shard_map/brh,brc->hc/dot_general | solution.py:56
  56.8 1.1 convolution_multiply_fusion
  58.0 0.0 copy-start.10
  58.0 0.0 copy-start.12
  58.0 0.0 copy-start.14
  58.0 1.0 convolution_bitcast_fusion.4
  59.1 1.0 multiply_reduce_fusion.7
  60.1 2.8 %collective-permute-start.6 = (f32[1,48,128]{2,1,0:T(8,128)S(1)}, f32[1,48,128]{2,1,0:T(8,128)S(1)}, u32[]{:S(2)}, u32[]{:S(2)}) collective-permute-start(f32[1,48,128]{2,1,0:T(8,128)S(1)} %get-tuple-element.40), channel_id=1, source_target_pairs={{0,4},{4,8},{8,12},{1,5},{5,9},{9,13},{2,6},{6,10},{10,14},{3,7},{... | collective-permute-start | bytes 73736 | tf_op jit(solution)/shard_map/ppermute | solution.py:17
  62.9 1.3 collective-permute-start.7
  64.2 0.7 pad_maximum_fusion.8
  65.0 0.7 pad_maximum_fusion.9
  65.7 0.0 all-reduce.4.cloned.1.call-update
  65.7 0.0 copy-start.15
  65.7 0.7 copy-done.15
  66.5 0.0 collective-permute-done.6
  66.5 1.0 collective-permute-done.7
  67.6 0.5 multiply_reduce_fusion.15
  68.1 36.3 %all-reduce = (f32[2,128]{1,0:T(2,128)}, f32[2,7,128]{2,1,0:T(8,128)S(1)}) all-reduce(f32[2,128]{1,0:T(2,128)S(1)} %pad_maximum_fusion.11, f32[2,7,128]{2,1,0:T(8,128)S(1)} %pad_maximum_fusion.10), channel_id=1, replica_groups=mesh['groups'=2,'ctx'=4,'dp'=2,'rep'=2] {'ctx','dp','rep'}, use_global_device_ids=true, to_apply=%region_6.7 | all-reduce | flops 2048 | bytes 16384 | tf_op jit(solution)/shard_map/psum | solution.py:111
  104.4 0.6 copy.11
  105.0 1.1 fusion.22
  106.1 55.6 %all-reduce.4.cloned.1.call-done = (f32[2,128,256]{2,1,0:T(8,128)}, f32[2,256,128]{2,1,0:T(8,128)}) async-done(((f32[2,128,256]{2,1,0:T(8,128)}, f32[2,256,128]{2,1,0:T(8,128)}), (f32[2,128,256]{2,1,0:T(8,128)}, f32[2,256,128]{2,1,0:T(8,128)})) %all-reduce.4.cloned.1.call-update) | async-done | bytes 524304 | tf_op jit(solution)/shard_map/psum | solution.py:111
  161.7 1.7 %copy.14 = f32[2,128,256]{2,1,0:T(8,128)} copy(f32[2,128,256]{2,1,0:T(8,128)} %get-tuple-element.71) | data formatting | bytes 524288
  163.4 0.7 copy.15
  (97 shorter events, 0.3 us)
Async XLA Ops:
  7.2 2.1 %copy-start = (f32[1,1024,128]{2,1,0:T(8,128)S(1)}, f32[1,1024,128]{2,1,0:T(8,128)}, u32[]{:S(2)}) copy-start(f32[1,1024,128]{2,1,0:T(8,128)} %param.6) | copy-start | bytes 1572868
  7.2 154.5 %all-reduce.4.cloned.1.call-start = ((), (), s32[]{:S(2)}) async-start(), calls=%async_computation | async-start | bytes 1048576 | tf_op jit(solution)/shard_map/psum | solution.py:111
  8.0 1.3 copy-start.16
  8.0 11.6 %copy-start.18 = (f32[128]{0:T(128)}, f32[128]{0:T(128)S(1)}, u32[]{:S(2)}) copy-start(f32[128]{0:T(128)S(1)} %get-tuple-element.62) | copy-start | bytes 1540
  9.5 6.0 %copy-start.20 = (f32[2,7,128]{2,0,1:T(2,128)S(1)}, f32[2,7,128]{2,0,1:T(2,128)}, u32[]{:S(2)}) copy-start(f32[2,7,128]{2,0,1:T(2,128)} %param.9) | copy-start | bytes 21508
  9.5 6.1 %collective-permute-start.1 = (f32[1,48,128]{2,1,0:T(8,128)S(1)}, f32[1,48,128]{2,1,0:T(8,128)S(1)}, u32[]{:S(2)}, u32[]{:S(2)}) collective-permute-start(f32[1,48,128]{2,1,0:T(8,128)S(1)} %get-tuple-element.46), channel_id=1, source_target_pairs={{4,0},{8,4},{12,8},{5,1},{9,5},{13,9},{6,2},{10,6},{14,10},{7,3},{... | collective-permute-start | bytes 73736 | tf_op jit(solution)/shard_map/ppermute | solution.py:20
  10.8 5.6 %collective-permute-start = (f32[1,48,128]{2,1,0:T(8,128)S(1)}, f32[1,48,128]{2,1,0:T(8,128)S(1)}, u32[]{:S(2)}, u32[]{:S(2)}) collective-permute-start(f32[1,48,128]{2,1,0:T(8,128)S(1)} %get-tuple-element.47), channel_id=1, source_target_pairs={{0,4},{4,8},{8,12},{1,5},{5,9},{9,13},{2,6},{6,10},{10,14},{3,7},{... | collective-permute-start | bytes 73736 | tf_op jit(solution)/shard_map/ppermute | solution.py:17
  15.5 0.9 copy-start.21
  15.5 0.9 copy-start.23
  15.5 0.9 copy-start.25
  15.5 0.9 copy-start.27
  15.5 0.9 copy-start.29
  15.6 0.9 copy-start.31
  15.6 0.9 copy-start.33
  15.6 16.4 %copy-start.35 = (f32[128]{0:T(128)}, f32[128]{0:T(128)S(1)}, u32[]{:S(2)}) copy-start(f32[128]{0:T(128)S(1)} %get-tuple-element.48) | copy-start | bytes 1540
  15.6 16.4 %copy-start.37 = (f32[128]{0:T(128)}, f32[128]{0:T(128)S(1)}, u32[]{:S(2)}) copy-start(f32[128]{0:T(128)S(1)} %get-tuple-element.49) | copy-start | bytes 1540
  15.6 16.4 %copy-start.39 = (f32[128]{0:T(128)}, f32[128]{0:T(128)S(1)}, u32[]{:S(2)}) copy-start(f32[128]{0:T(128)S(1)} %get-tuple-element.50) | copy-start | bytes 1540
  15.6 16.4 %copy-start.41 = (f32[128]{0:T(128)}, f32[128]{0:T(128)S(1)}, u32[]{:S(2)}) copy-start(f32[128]{0:T(128)S(1)} %get-tuple-element.51) | copy-start | bytes 1540
  15.6 16.4 %copy-start.43 = (f32[128]{0:T(128)}, f32[128]{0:T(128)S(1)}, u32[]{:S(2)}) copy-start(f32[128]{0:T(128)S(1)} %get-tuple-element.58) | copy-start | bytes 1540
  15.6 16.4 %copy-start.45 = (f32[128]{0:T(128)}, f32[128]{0:T(128)S(1)}, u32[]{:S(2)}) copy-start(f32[128]{0:T(128)S(1)} %get-tuple-element.60) | copy-start | bytes 1540
  15.6 16.4 %copy-start.47 = (f32[128]{0:T(128)}, f32[128]{0:T(128)S(1)}, u32[]{:S(2)}) copy-start(f32[128]{0:T(128)S(1)} %get-tuple-element.61) | copy-start | bytes 1540
  15.7 1.1 copy-start.11
  16.4 0.6 copy-start.13
  16.5 1.0 copy-start.9
  17.4 1.0 copy-start.49
  18.4 1.2 copy-start.1
  19.9 11.2 %collective-permute-start.3 = (f32[1,768,128]{2,1,0:T(8,128)S(1)}, f32[1,768,128]{2,1,0:T(8,128)S(1)}, u32[]{:S(2)}, u32[]{:S(2)}) collective-permute-start(f32[1,768,128]{2,1,0:T(8,128)S(1)} %get-tuple-element.44), channel_id=1, source_target_pairs={{4,0},{8,4},{12,8},{5,1},{9,5},{13,9},{6,2},{10,6},{14,10},{7,3},{... | collective-permute-start | bytes 1179656 | tf_op jit(solution)/shard_map/ppermute | solution.py:20
  21.2 10.8 %collective-permute-start.2 = (f32[1,768,128]{2,1,0:T(8,128)S(1)}, f32[1,768,128]{2,1,0:T(8,128)S(1)}, u32[]{:S(2)}, u32[]{:S(2)}) collective-permute-start(f32[1,768,128]{2,1,0:T(8,128)S(1)} %get-tuple-element.45), channel_id=1, source_target_pairs={{0,4},{4,8},{8,12},{1,5},{5,9},{9,13},{2,6},{6,10},{10,14},{3,7},{... | collective-permute-start | bytes 1179656 | tf_op jit(solution)/shard_map/ppermute | solution.py:17
  32.3 2.0 %copy-start.6 = (f32[1,1024,128]{2,1,0:T(8,128)S(1)}, f32[1,1024,128]{2,1,0:T(8,128)}, u32[]{:S(2)}) copy-start(f32[1,1024,128]{2,1,0:T(8,128)} %param.7) | copy-start | bytes 1572868
  33.3 1.0 copy-start.3
  35.4 1.7 %copy-start.5 = (f32[1024,256]{1,0:T(8,128)}, f32[1024,256]{1,0:T(8,128)S(1)}, u32[]{:S(2)}) copy-start(f32[1024,256]{1,0:T(8,128)S(1)} %convolution_multiply_fusion.1) | copy-start | bytes 3145732
  38.1 11.3 %collective-permute-start.4 = (f32[1,768,128]{2,1,0:T(8,128)}, f32[1,768,128]{2,1,0:T(8,128)S(1)}, u32[]{:S(2)}, u32[]{:S(2)}) collective-permute-start(f32[1,768,128]{2,1,0:T(8,128)} %get-tuple-element.42), channel_id=1, source_target_pairs={{0,4},{4,8},{8,12},{1,5},{5,9},{9,13},{2,6},{6,10},{10,14},{3,7},{... | collective-permute-start | bytes 1179656 | tf_op jit(solution)/shard_map/ppermute | solution.py:17
  42.2 9.8 %collective-permute-start.5 = (f32[1,768,128]{2,1,0:T(8,128)}, f32[1,768,128]{2,1,0:T(8,128)}, u32[]{:S(2)}, u32[]{:S(2)}) collective-permute-start(f32[1,768,128]{2,1,0:T(8,128)} %get-tuple-element.43), channel_id=1, source_target_pairs={{4,0},{8,4},{12,8},{5,1},{9,5},{13,9},{6,2},{10,6},{14,10},{7,3},{... | collective-permute-start | bytes 1179656 | tf_op jit(solution)/shard_map/ppermute | solution.py:20
  45.0 2.4 %copy-start.4 = (f32[1024,256]{1,0:T(8,128)S(1)}, f32[1024,256]{1,0:T(8,128)}, u32[]{:S(2)}) copy-start(f32[1024,256]{1,0:T(8,128)} %copy-done.3) | copy-start | bytes 3145732
  45.0 2.4 %copy-start.7 = (f32[1,1024,128]{2,1,0:T(8,128)S(1)}, f32[1,1024,128]{2,1,0:T(8,128)}, u32[]{:S(2)}) copy-start(f32[1,1024,128]{2,1,0:T(8,128)} %param.7) | copy-start | bytes 1572868
  47.4 4.6 %copy-start.19 = (f32[128]{0:T(128)S(1)}, f32[128]{0:T(128)}, u32[]{:S(2)}) copy-start(f32[128]{0:T(128)} %copy-done.18) | copy-start | bytes 1540
  47.4 4.6 %copy-start.36 = (f32[128]{0:T(128)S(1)}, f32[128]{0:T(128)}, u32[]{:S(2)}) copy-start(f32[128]{0:T(128)} %copy-done.35) | copy-start | bytes 1540
  47.4 4.6 %copy-start.38 = (f32[128]{0:T(128)S(1)}, f32[128]{0:T(128)}, u32[]{:S(2)}) copy-start(f32[128]{0:T(128)} %copy-done.37) | copy-start | bytes 1540
  47.4 4.6 %copy-start.40 = (f32[128]{0:T(128)S(1)}, f32[128]{0:T(128)}, u32[]{:S(2)}) copy-start(f32[128]{0:T(128)} %copy-done.39) | copy-start | bytes 1540
  47.4 4.6 %copy-start.42 = (f32[128]{0:T(128)S(1)}, f32[128]{0:T(128)}, u32[]{:S(2)}) copy-start(f32[128]{0:T(128)} %copy-done.41) | copy-start | bytes 1540
  47.4 4.6 %copy-start.44 = (f32[128]{0:T(128)S(1)}, f32[128]{0:T(128)}, u32[]{:S(2)}) copy-start(f32[128]{0:T(128)} %copy-done.43) | copy-start | bytes 1540
  47.4 4.6 %copy-start.46 = (f32[128]{0:T(128)S(1)}, f32[128]{0:T(128)}, u32[]{:S(2)}) copy-start(f32[128]{0:T(128)} %copy-done.45) | copy-start | bytes 1540
  47.4 4.6 %copy-start.48 = (f32[128]{0:T(128)S(1)}, f32[128]{0:T(128)}, u32[]{:S(2)}) copy-start(f32[128]{0:T(128)} %copy-done.47) | copy-start | bytes 1540
  53.7 1.2 copy-start.2
  54.9 1.9 %copy-start.50 = (f32[2,256,128]{2,1,0:T(8,128)S(1)}, f32[2,256,128]{2,1,0:T(8,128)}, u32[]{:S(2)}) copy-start(f32[2,256,128]{2,1,0:T(8,128)} %param.11) | copy-start | bytes 786436
  58.0 1.1 copy-start.10
  58.0 1.1 copy-start.12
  58.0 1.1 copy-start.14
  60.1 6.3 %collective-permute-start.6 = (f32[1,48,128]{2,1,0:T(8,128)S(1)}, f32[1,48,128]{2,1,0:T(8,128)S(1)}, u32[]{:S(2)}, u32[]{:S(2)}) collective-permute-start(f32[1,48,128]{2,1,0:T(8,128)S(1)} %get-tuple-element.40), channel_id=1, source_target_pairs={{0,4},{4,8},{8,12},{1,5},{5,9},{9,13},{2,6},{6,10},{10,14},{3,7},{... | collective-permute-start | bytes 73736 | tf_op jit(solution)/shard_map/ppermute | solution.py:17
  62.9 4.6 %collective-permute-start.7 = (f32[1,48,128]{2,1,0:T(8,128)S(1)}, f32[1,48,128]{2,1,0:T(8,128)S(1)}, u32[]{:S(2)}, u32[]{:S(2)}) collective-permute-start(f32[1,48,128]{2,1,0:T(8,128)S(1)} %get-tuple-element.41), channel_id=1, source_target_pairs={{4,0},{8,4},{12,8},{5,1},{9,5},{13,9},{6,2},{10,6},{14,10},{7,3},{... | collective-permute-start | bytes 73736 | tf_op jit(solution)/shard_map/ppermute | solution.py:20
  65.7 0.7 copy-start.15
  66.4 1.1 copy-start.17
  66.4 1.1 copy-start.22
  66.4 1.1 copy-start.24
  66.4 1.1 copy-start.26
  66.4 1.1 copy-start.28
  66.4 1.1 copy-start.30
  66.4 1.1 copy-start.32
  66.4 1.1 copy-start.34
  161.7 1.7 %copy-start.8 = (f32[2,256,128]{2,1,0:T(8,128)S(1)}, f32[2,256,128]{2,1,0:T(8,128)}, u32[]{:S(2)}) copy-start(f32[2,256,128]{2,1,0:T(8,128)} %get-tuple-element.72) | copy-start | bytes 786436
Sparse Core Ops, SparseCore 0:
  65.8 95.8 all-reduce.3
where the time goes:
time: 172 us; the launch traced here: 171 us
  waiting for transfers between devices  66.6 us (39%)
  blocking collectives  36.3 us (21%)
  starting transfers between devices  21.3 us (12%)
  matrix products  15.3 us (9%)
  between operations  14.9 us (9%)
  local copies, waits for them, and re-layouts  9.53 us (6%)
  other arithmetic  7.23 us (4%)
    psum x1, waiting for transfers between devices, local(): lax.psum((gain_total, taps_total, input_weight_sum, wout_total), ('ctx',...  55.6 us
    psum x1, blocking collectives, local(): lax.psum((gain_total, taps_total, input_weight_sum, wout_total), ('ctx',...  36.3 us
    ppermute x4, starting transfers between devices, with_halo(): lax.ppermute(lax.slice_in_dim(block, block.shape[dim] - width, None, axis...  15.9 us
    ppermute x4, waiting for transfers between devices, with_halo(): lax.ppermute(lax.slice_in_dim(block, 0, width, axis=dim), axis, backward)  9.29 us
    unnamed x105, local copies, waits for them, and re-layouts  6.46 us
    ppermute x4, starting transfers between devices, with_halo(): lax.ppermute(lax.slice_in_dim(block, 0, width, axis=dim), axis, backward)  5.35 us
    dot_general x2, matrix products, backward_block(): jnp.einsum('brh,brc->hc', act_out, grad_out, precision=lax.Precision.HIGH...  3.78 us
  transfers between devices with their start and end apart: 9, of which 6 were waited for; matrix products, arithmetic and copies ran while one was open for 5% of the time, Pallas kernels for 0%

commit v1 on v0

--- a/solution.py
+++ b/solution.py
@@ -109,7 +109,7 @@
     input_weight_sum = jnp.stack([block_grads[index_b][2] for index_b in range(BLOCKS)])
     wout_total = jnp.stack([block_grads[index_b][3] for index_b in range(BLOCKS)])
     gain_total, taps_total, input_weight_sum, wout_total = lax.psum(
-        (gain_total, taps_total, input_weight_sum, wout_total), ("ctx", "dp", "rep")
+        lax.psum((gain_total, taps_total, input_weight_sum, wout_total), ("dp", "rep")), "ctx"
     )
     return (grad_flow, gain_total, taps_total, input_weight_sum, wout_total)
 

time: 172 us -> 156 us (0.907)
  blocking collectives: 36.3 us -> 18.3 us
    psum x1 -> x2, blocking collectives: 36.3 us -> 18.3 us  [the longest x1 11.1 us: local(): lax.psum(lax.psum((gain_total, taps_total, input_weight_sum, wout_total),...]
    psum x1 -> x2, waiting for transfers between devices: 55.6 us -> 56.4 us  [the longest x1 34.8 us: local(): lax.psum((gain_total, taps_total, input_weight_sum, wout_total), ('dp', '...]
  transfers between devices with their start and end apart: 9 -> 10, of which waited for: 6 -> 7; matrix products, arithmetic and copies ran while one was open for 5% -> 6% of each run, Pallas kernels for 0% -> 0%
where the time goes in v1:
time: 156 us; the launch traced here: 154 us
  waiting for transfers between devices  67.3 us (43%)
  starting transfers between devices  21.3 us (14%)
  blocking collectives  18.3 us (12%)
  matrix products  15.3 us (10%)
  between operations  14.9 us (10%)
  local copies, waits for them, and re-layouts  9.53 us (6%)
  other arithmetic  7.23 us (5%)
    psum x1, waiting for transfers between devices, local(): lax.psum((gain_total, taps_total, input_weight_sum, wout_total), ('dp', '...  34.8 us
    psum x1, waiting for transfers between devices, local(): lax.psum(lax.psum((gain_total, taps_total, input_weight_sum, wout_total),...  21.7 us
    ppermute x4, starting transfers between devices, with_halo(): lax.ppermute(lax.slice_in_dim(block, block.shape[dim] - width, None, axis...  15.9 us
    psum x1, blocking collectives, local(): lax.psum(lax.psum((gain_total, taps_total, input_weight_sum, wout_total),...  11.1 us
    ppermute x4, waiting for transfers between devices, with_halo(): lax.ppermute(lax.slice_in_dim(block, 0, width, axis=dim), axis, backward)  9.24 us
    psum x1, blocking collectives, local(): lax.psum((gain_total, taps_total, input_weight_sum, wout_total), ('dp', '...  7.13 us
    unnamed x105, local copies, waits for them, and re-layouts  6.46 us
    ppermute x4, starting transfers between devices, with_halo(): lax.ppermute(lax.slice_in_dim(block, 0, width, axis=dim), axis, backward)  5.35 us
  transfers between devices with their start and end apart: 10, of which 7 were waited for; matrix products, arithmetic and copies ran while one was open for 6% of the time, Pallas kernels for 0%

profile of v1, /device:TPU:1, one launch (start us, length us, event | category | flops | bytes accessed | tf_op | source)
XLA Modules:
  0.0 153.8 jit_solution(11035074428236820447)
XLA Ops:
  7.2 0.0 copy-start
  7.2 0.0 all-reduce.7.cloned.1.call-start
  7.2 0.8 slice_bitcast_fusion.5
  8.0 1.2 multiply_reduce_fusion.19
  9.3 0.2 multiply_multiply_fusion.1
  9.5 0.0 copy-start.20
  9.5 1.3 collective-permute-start.1
  10.8 4.7 %collective-permute-start = (f32[1,48,128]{2,1,0:T(8,128)S(1)}, f32[1,48,128]{2,1,0:T(8,128)S(1)}, u32[]{:S(2)}, u32[]{:S(2)}) collective-permute-start(f32[1,48,128]{2,1,0:T(8,128)S(1)} %get-tuple-element.51), channel_id=1, source_target_pairs={{0,4},{4,8},{8,12},{1,5},{5,9},{9,13},{2,6},{6,10},{10,14},{3,7},{... | collective-permute-start | bytes 73736 | tf_op jit(solution)/shard_map/ppermute | solution.py:17
  15.7 0.0 copy-start.11
  15.7 0.7 collective-permute-done
  16.5 0.0 copy-start.9
  16.5 0.2 multiply_add_fusion.1
  16.7 0.3 copy-done.13
  17.0 0.4 copy-done.9
  17.4 1.0 fusion.51
  18.4 1.2 multiply_reduce_fusion.18
  19.6 0.2 multiply_multiply_fusion
  19.8 0.1 fusion.83
  19.9 1.3 collective-permute-start.3
  21.2 4.3 %collective-permute-start.2 = (f32[1,768,128]{2,1,0:T(8,128)S(1)}, f32[1,768,128]{2,1,0:T(8,128)S(1)}, u32[]{:S(2)}, u32[]{:S(2)}) collective-permute-start(f32[1,768,128]{2,1,0:T(8,128)S(1)} %get-tuple-element.49), channel_id=1, source_target_pairs={{0,4},{4,8},{8,12},{1,5},{5,9},{9,13},{2,6},{6,10},{10,14},{3,7},{... | collective-permute-start | bytes 1179656 | tf_op jit(solution)/shard_map/ppermute | solution.py:17
  25.5 5.6 %collective-permute-done.3 = f32[1,768,128]{2,1,0:T(8,128)S(1)} collective-permute-done((f32[1,768,128]{2,1,0:T(8,128)S(1)}, f32[1,768,128]{2,1,0:T(8,128)S(1)}, u32[]{:S(2)}, u32[]{:S(2)}) %collective-permute-start.3) | collective-permute-done | bytes 393248 | tf_op jit(solution)/shard_map/ppermute | solution.py:20
  31.1 0.9 collective-permute-done.2
  32.1 0.2 multiply_add_fusion
  32.3 0.0 copy-start.6
  32.3 1.0 fusion.48
  33.3 1.0 copy-done.3
  34.3 1.1 convolution_multiply_fusion.1
  35.4 1.7 %multiply_reduce_fusion = (f32[128]{0:T(128)}, f32[128]{0:T(128)}, f32[128]{0:T(128)}, f32[128]{0:T(128)}, f32[128]{0:T(128)}, /*index=5*/f32[128]{0:T(128)}, f32[128]{0:T(128)}, f32[1024,128]{1,0:T(8,128)S(1)}) fusion(f32[1,768,128]{2,1,0:T(8,128)S(1)} %collective-permute-done.3, f32[1,1024,128]{2,1,0:T(8,128)S(1)} %multiply_multiply_fusion, ...), kind=kOutput, calls=%fused_computation.106 | convolution fusion | flops 405273728 | bytes 3018240 | tf_op jit(solution)/shard_map/brh,ch->brc/dot_general | solution.py:63
  37.1 0.9 fusion.82
  38.1 4.1 %collective-permute-start.4 = (f32[1,768,128]{2,1,0:T(8,128)}, f32[1,768,128]{2,1,0:T(8,128)S(1)}, u32[]{:S(2)}, u32[]{:S(2)}) collective-permute-start(f32[1,768,128]{2,1,0:T(8,128)} %get-tuple-element.46), channel_id=1, source_target_pairs={{0,4},{4,8},{8,12},{1,5},{5,9},{9,13},{2,6},{6,10},{10,14},{3,7},{... | collective-permute-start | bytes 1179656 | tf_op jit(solution)/shard_map/ppermute | solution.py:17
  42.2 1.5 collective-permute-start.5
  43.7 1.3 stack.103
  45.0 2.4 %convolution_bitcast_fusion.3 = f32[1,128,256]{2,1,0:T(8,128)S(1)} fusion(f32[1024,256]{1,0:T(8,128)} %copy-done.5, f32[1,1024,128]{2,1,0:T(8,128)S(1)} %multiply_add_fusion), kind=kOutput, calls=%fused_computation.6 | convolution fusion | flops 402653184 | bytes 1703936 | tf_op jit(solution)/shard_map/brc,brh->ch/dot_general | solution.py:62
  47.4 0.0 copy-start.19
  47.5 1.9 %convolution_bitcast_fusion.1 = f32[1,256,128]{2,1,0:T(8,128)S(1)} fusion(f32[1024,256]{1,0:T(8,128)S(1)} %copy-done.4, f32[1,1024,128]{2,1,0:T(8,128)S(1)} %copy-done.7), kind=kOutput, calls=%fused_computation.4 | convolution fusion | flops 403701760 | bytes 1703936 | tf_op jit(solution)/shard_map/brh,brc->hc/dot_general | solution.py:56
  49.4 2.6 %collective-permute-done.5 = f32[1,768,128]{2,1,0:T(8,128)} collective-permute-done((f32[1,768,128]{2,1,0:T(8,128)}, f32[1,768,128]{2,1,0:T(8,128)}, u32[]{:S(2)}, u32[]{:S(2)}) %collective-permute-start.5) | collective-permute-done | bytes 393248 | tf_op jit(solution)/shard_map/ppermute | solution.py:20
  52.0 1.7 %multiply_reduce_fusion.14 = (f32[128]{0:T(128)S(1)}, f32[1024]{0:T(1024)S(1)}, f32[1,1024,128]{2,1,0:T(8,128)S(1)}) fusion(f32[1,1024,128]{2,1,0:T(8,128)S(1)} %get-tuple-element.69, f32[1024]{0:T(1024)S(1)} %fusion.75, f32[128]{0:T(128)S(1)} %copy-done.19, f32[1,768,128]{2,1,0:T(8,128)} %collective-permute-done.5, f32[1,1024,128]{2,1,0:T(8,128)S(1)} %bitcast.133, ...), kind=kLoop, calls=%fused_computation.120 | loop fusion | flops 3275648 | bytes 2896384 | tf_op jit(solution)/shard_map/transpose(jvp())/reduce_sum | solution.py:27
  53.7 0.3 fusion.21
  54.1 0.9 copy-done.2
  54.9 1.9 %convolution_bitcast_fusion.2 = f32[1,256,128]{2,1,0:T(8,128)S(1)} fusion(f32[1,1024,128]{2,1,0:T(8,128)S(1)} %fusion.21, f32[1024,256]{1,0:T(8,128)S(1)} %copy-done.2), kind=kOutput, calls=%fused_computation.5 | convolution fusion | flops 403701760 | bytes 1703936 | tf_op jit(solution)/shard_map/brh,brc->hc/dot_general | solution.py:56
  56.8 1.1 convolution_multiply_fusion
  58.0 0.0 copy-start.10
  58.0 0.0 copy-start.12
  58.0 0.0 copy-start.14
  58.0 1.0 convolution_bitcast_fusion.4
  59.1 1.0 multiply_reduce_fusion.7
  60.1 2.8 %collective-permute-start.6 = (f32[1,48,128]{2,1,0:T(8,128)S(1)}, f32[1,48,128]{2,1,0:T(8,128)S(1)}, u32[]{:S(2)}, u32[]{:S(2)}) collective-permute-start(f32[1,48,128]{2,1,0:T(8,128)S(1)} %get-tuple-element.44), channel_id=1, source_target_pairs={{0,4},{4,8},{8,12},{1,5},{5,9},{9,13},{2,6},{6,10},{10,14},{3,7},{... | collective-permute-start | bytes 73736 | tf_op jit(solution)/shard_map/ppermute | solution.py:17
  62.9 1.3 collective-permute-start.7
  64.2 0.7 pad_maximum_fusion.8
  65.0 0.7 pad_maximum_fusion.9
  65.7 0.0 all-reduce.7.cloned.1.call-update
  65.7 0.0 all-reduce.9.cloned.1.call-start
  65.8 0.7 copy-done.15
  66.5 1.0 collective-permute-done.7
  67.6 0.5 multiply_reduce_fusion.15
  68.1 34.8 %all-reduce.7.cloned.1.call-done = (f32[2,128,256]{2,1,0:T(8,128)}, f32[2,256,128]{2,1,0:T(8,128)}) async-done(((f32[2,128,256]{2,1,0:T(8,128)}, f32[2,256,128]{2,1,0:T(8,128)}), (f32[2,128,256]{2,1,0:T(8,128)}, f32[2,256,128]{2,1,0:T(8,128)})) %all-reduce.7.cloned.1.call-update) | async-done | bytes 524304 | tf_op jit(solution)/shard_map/psum | solution.py:112
  102.8 0.0 all-reduce.9.cloned.1.call-update
  102.9 7.1 %all-reduce = (f32[2,128]{1,0:T(2,128)S(1)}, f32[2,7,128]{2,1,0:T(8,128)S(1)}) all-reduce(f32[2,128]{1,0:T(2,128)S(1)} %pad_maximum_fusion.11, f32[2,7,128]{2,1,0:T(8,128)S(1)} %pad_maximum_fusion.10), channel_id=1, replica_groups=mesh['groups'=2,'ctx'=4,'dp'=2,'rep'=2] {'dp','rep'}, use_global_device_ids=true, to_apply=%region_6.7 | all-reduce | flops 2048 | bytes 16384 | tf_op jit(solution)/shard_map/psum | solution.py:112
  110.0 11.1 %all-reduce.2 = (f32[2,128]{1,0:T(2,128)}, f32[2,7,128]{2,1,0:T(8,128)S(1)}) all-reduce(f32[2,128]{1,0:T(2,128)S(1)} %get-tuple-element.34, f32[2,7,128]{2,1,0:T(8,128)S(1)} %get-tuple-element.35), channel_id=1, replica_groups=mesh['groups'=2,'ctx'=4,'dp'=2,'rep'=2] {'ctx'}, use_global_device_ids=true, to_apply=%region_7.8 | all-reduce | flops 2048 | bytes 16384 | tf_op jit(solution)/shard_map/psum | solution.py:111
  121.1 0.6 copy.11
  121.7 1.1 fusion.22
  122.9 21.7 %all-reduce.9.cloned.1.call-done = (f32[2,128,256]{2,1,0:T(8,128)}, f32[2,256,128]{2,1,0:T(8,128)}) async-done(((f32[2,128,256]{2,1,0:T(8,128)}, f32[2,256,128]{2,1,0:T(8,128)}), (f32[2,128,256]{2,1,0:T(8,128)}, f32[2,256,128]{2,1,0:T(8,128)})) %all-reduce.9.cloned.1.call-update) | async-done | bytes 524304 | tf_op jit(solution)/shard_map/psum | solution.py:111
  144.5 1.7 %copy.16 = f32[2,128,256]{2,1,0:T(8,128)} copy(f32[2,128,256]{2,1,0:T(8,128)} %get-tuple-element.75) | data formatting | bytes 524288
  146.2 0.7 copy.17
  (101 shorter events, 0.3 us)
Async XLA Ops:
  7.2 2.1 %copy-start = (f32[1,1024,128]{2,1,0:T(8,128)S(1)}, f32[1,1024,128]{2,1,0:T(8,128)}, u32[]{:S(2)}) copy-start(f32[1,1024,128]{2,1,0:T(8,128)} %param.6) | copy-start | bytes 1572868
  7.2 95.6 %all-reduce.7.cloned.1.call-start = ((), (), s32[]{:S(2)}) async-start(), calls=%async_computation | async-start | bytes 1048576 | tf_op jit(solution)/shard_map/psum | solution.py:112
  8.0 1.3 copy-start.16
  8.0 11.6 %copy-start.18 = (f32[128]{0:T(128)}, f32[128]{0:T(128)S(1)}, u32[]{:S(2)}) copy-start(f32[128]{0:T(128)S(1)} %get-tuple-element.66) | copy-start | bytes 1540
  9.5 6.0 %copy-start.20 = (f32[2,7,128]{2,0,1:T(2,128)S(1)}, f32[2,7,128]{2,0,1:T(2,128)}, u32[]{:S(2)}) copy-start(f32[2,7,128]{2,0,1:T(2,128)} %param.9) | copy-start | bytes 21508
  9.5 6.1 %collective-permute-start.1 = (f32[1,48,128]{2,1,0:T(8,128)S(1)}, f32[1,48,128]{2,1,0:T(8,128)S(1)}, u32[]{:S(2)}, u32[]{:S(2)}) collective-permute-start(f32[1,48,128]{2,1,0:T(8,128)S(1)} %get-tuple-element.50), channel_id=1, source_target_pairs={{4,0},{8,4},{12,8},{5,1},{9,5},{13,9},{6,2},{10,6},{14,10},{7,3},{... | collective-permute-start | bytes 73736 | tf_op jit(solution)/shard_map/ppermute | solution.py:20
  10.8 5.6 %collective-permute-start = (f32[1,48,128]{2,1,0:T(8,128)S(1)}, f32[1,48,128]{2,1,0:T(8,128)S(1)}, u32[]{:S(2)}, u32[]{:S(2)}) collective-permute-start(f32[1,48,128]{2,1,0:T(8,128)S(1)} %get-tuple-element.51), channel_id=1, source_target_pairs={{0,4},{4,8},{8,12},{1,5},{5,9},{9,13},{2,6},{6,10},{10,14},{3,7},{... | collective-permute-start | bytes 73736 | tf_op jit(solution)/shard_map/ppermute | solution.py:17
  15.5 0.9 copy-start.21
  15.5 0.9 copy-start.23
  15.5 0.9 copy-start.25
  15.5 0.9 copy-start.27
  15.5 0.9 copy-start.29
  15.6 0.9 copy-start.31
  15.6 0.9 copy-start.33
  15.6 16.4 %copy-start.35 = (f32[128]{0:T(128)}, f32[128]{0:T(128)S(1)}, u32[]{:S(2)}) copy-start(f32[128]{0:T(128)S(1)} %get-tuple-element.52) | copy-start | bytes 1540
  15.6 16.4 %copy-start.37 = (f32[128]{0:T(128)}, f32[128]{0:T(128)S(1)}, u32[]{:S(2)}) copy-start(f32[128]{0:T(128)S(1)} %get-tuple-element.53) | copy-start | bytes 1540
  15.6 16.4 %copy-start.39 = (f32[128]{0:T(128)}, f32[128]{0:T(128)S(1)}, u32[]{:S(2)}) copy-start(f32[128]{0:T(128)S(1)} %get-tuple-element.54) | copy-start | bytes 1540
  15.6 16.4 %copy-start.41 = (f32[128]{0:T(128)}, f32[128]{0:T(128)S(1)}, u32[]{:S(2)}) copy-start(f32[128]{0:T(128)S(1)} %get-tuple-element.55) | copy-start | bytes 1540
  15.6 16.4 %copy-start.43 = (f32[128]{0:T(128)}, f32[128]{0:T(128)S(1)}, u32[]{:S(2)}) copy-start(f32[128]{0:T(128)S(1)} %get-tuple-element.62) | copy-start | bytes 1540
  15.6 16.4 %copy-start.45 = (f32[128]{0:T(128)}, f32[128]{0:T(128)S(1)}, u32[]{:S(2)}) copy-start(f32[128]{0:T(128)S(1)} %get-tuple-element.64) | copy-start | bytes 1540
  15.6 16.4 %copy-start.47 = (f32[128]{0:T(128)}, f32[128]{0:T(128)S(1)}, u32[]{:S(2)}) copy-start(f32[128]{0:T(128)S(1)} %get-tuple-element.65) | copy-start | bytes 1540
  15.7 1.1 copy-start.11
  16.4 0.6 copy-start.13
  16.5 1.0 copy-start.9
  17.4 1.0 copy-start.49
  18.4 1.2 copy-start.1
  19.9 11.2 %collective-permute-start.3 = (f32[1,768,128]{2,1,0:T(8,128)S(1)}, f32[1,768,128]{2,1,0:T(8,128)S(1)}, u32[]{:S(2)}, u32[]{:S(2)}) collective-permute-start(f32[1,768,128]{2,1,0:T(8,128)S(1)} %get-tuple-element.48), channel_id=1, source_target_pairs={{4,0},{8,4},{12,8},{5,1},{9,5},{13,9},{6,2},{10,6},{14,10},{7,3},{... | collective-permute-start | bytes 1179656 | tf_op jit(solution)/shard_map/ppermute | solution.py:20
  21.2 10.8 %collective-permute-start.2 = (f32[1,768,128]{2,1,0:T(8,128)S(1)}, f32[1,768,128]{2,1,0:T(8,128)S(1)}, u32[]{:S(2)}, u32[]{:S(2)}) collective-permute-start(f32[1,768,128]{2,1,0:T(8,128)S(1)} %get-tuple-element.49), channel_id=1, source_target_pairs={{0,4},{4,8},{8,12},{1,5},{5,9},{9,13},{2,6},{6,10},{10,14},{3,7},{... | collective-permute-start | bytes 1179656 | tf_op jit(solution)/shard_map/ppermute | solution.py:17
  32.3 2.0 %copy-start.6 = (f32[1,1024,128]{2,1,0:T(8,128)S(1)}, f32[1,1024,128]{2,1,0:T(8,128)}, u32[]{:S(2)}) copy-start(f32[1,1024,128]{2,1,0:T(8,128)} %param.7) | copy-start | bytes 1572868
  33.3 1.0 copy-start.3
  35.4 1.7 %copy-start.5 = (f32[1024,256]{1,0:T(8,128)}, f32[1024,256]{1,0:T(8,128)S(1)}, u32[]{:S(2)}) copy-start(f32[1024,256]{1,0:T(8,128)S(1)} %convolution_multiply_fusion.1) | copy-start | bytes 3145732
  38.1 11.3 %collective-permute-start.4 = (f32[1,768,128]{2,1,0:T(8,128)}, f32[1,768,128]{2,1,0:T(8,128)S(1)}, u32[]{:S(2)}, u32[]{:S(2)}) collective-permute-start(f32[1,768,128]{2,1,0:T(8,128)} %get-tuple-element.46), channel_id=1, source_target_pairs={{0,4},{4,8},{8,12},{1,5},{5,9},{9,13},{2,6},{6,10},{10,14},{3,7},{... | collective-permute-start | bytes 1179656 | tf_op jit(solution)/shard_map/ppermute | solution.py:17
  42.2 9.8 %collective-permute-start.5 = (f32[1,768,128]{2,1,0:T(8,128)}, f32[1,768,128]{2,1,0:T(8,128)}, u32[]{:S(2)}, u32[]{:S(2)}) collective-permute-start(f32[1,768,128]{2,1,0:T(8,128)} %get-tuple-element.47), channel_id=1, source_target_pairs={{4,0},{8,4},{12,8},{5,1},{9,5},{13,9},{6,2},{10,6},{14,10},{7,3},{... | collective-permute-start | bytes 1179656 | tf_op jit(solution)/shard_map/ppermute | solution.py:20
  45.0 2.4 %copy-start.4 = (f32[1024,256]{1,0:T(8,128)S(1)}, f32[1024,256]{1,0:T(8,128)}, u32[]{:S(2)}) copy-start(f32[1024,256]{1,0:T(8,128)} %copy-done.3) | copy-start | bytes 3145732
  45.0 2.4 %copy-start.7 = (f32[1,1024,128]{2,1,0:T(8,128)S(1)}, f32[1,1024,128]{2,1,0:T(8,128)}, u32[]{:S(2)}) copy-start(f32[1,1024,128]{2,1,0:T(8,128)} %param.7) | copy-start | bytes 1572868
  47.4 4.6 %copy-start.19 = (f32[128]{0:T(128)S(1)}, f32[128]{0:T(128)}, u32[]{:S(2)}) copy-start(f32[128]{0:T(128)} %copy-done.18) | copy-start | bytes 1540
  47.4 4.6 %copy-start.36 = (f32[128]{0:T(128)S(1)}, f32[128]{0:T(128)}, u32[]{:S(2)}) copy-start(f32[128]{0:T(128)} %copy-done.35) | copy-start | bytes 1540
  47.4 4.6 %copy-start.38 = (f32[128]{0:T(128)S(1)}, f32[128]{0:T(128)}, u32[]{:S(2)}) copy-start(f32[128]{0:T(128)} %copy-done.37) | copy-start | bytes 1540
  47.4 4.6 %copy-start.40 = (f32[128]{0:T(128)S(1)}, f32[128]{0:T(128)}, u32[]{:S(2)}) copy-start(f32[128]{0:T(128)} %copy-done.39) | copy-start | bytes 1540
  47.4 4.6 %copy-start.42 = (f32[128]{0:T(128)S(1)}, f32[128]{0:T(128)}, u32[]{:S(2)}) copy-start(f32[128]{0:T(128)} %copy-done.41) | copy-start | bytes 1540
  47.4 4.6 %copy-start.44 = (f32[128]{0:T(128)S(1)}, f32[128]{0:T(128)}, u32[]{:S(2)}) copy-start(f32[128]{0:T(128)} %copy-done.43) | copy-start | bytes 1540
  47.4 4.6 %copy-start.46 = (f32[128]{0:T(128)S(1)}, f32[128]{0:T(128)}, u32[]{:S(2)}) copy-start(f32[128]{0:T(128)} %copy-done.45) | copy-start | bytes 1540
  47.4 4.6 %copy-start.48 = (f32[128]{0:T(128)S(1)}, f32[128]{0:T(128)}, u32[]{:S(2)}) copy-start(f32[128]{0:T(128)} %copy-done.47) | copy-start | bytes 1540
  53.7 1.2 copy-start.2
  54.9 1.9 %copy-start.50 = (f32[2,256,128]{2,1,0:T(8,128)S(1)}, f32[2,256,128]{2,1,0:T(8,128)}, u32[]{:S(2)}) copy-start(f32[2,256,128]{2,1,0:T(8,128)} %param.11) | copy-start | bytes 786436
  58.0 1.1 copy-start.10
  58.0 1.1 copy-start.12
  58.0 1.1 copy-start.14
  60.1 6.4 %collective-permute-start.6 = (f32[1,48,128]{2,1,0:T(8,128)S(1)}, f32[1,48,128]{2,1,0:T(8,128)S(1)}, u32[]{:S(2)}, u32[]{:S(2)}) collective-permute-start(f32[1,48,128]{2,1,0:T(8,128)S(1)} %get-tuple-element.44), channel_id=1, source_target_pairs={{0,4},{4,8},{8,12},{1,5},{5,9},{9,13},{2,6},{6,10},{10,14},{3,7},{... | collective-permute-start | bytes 73736 | tf_op jit(solution)/shard_map/ppermute | solution.py:17
  62.9 4.6 %collective-permute-start.7 = (f32[1,48,128]{2,1,0:T(8,128)S(1)}, f32[1,48,128]{2,1,0:T(8,128)S(1)}, u32[]{:S(2)}, u32[]{:S(2)}) collective-permute-start(f32[1,48,128]{2,1,0:T(8,128)S(1)} %get-tuple-element.45), channel_id=1, source_target_pairs={{4,0},{8,4},{12,8},{5,1},{9,5},{13,9},{6,2},{10,6},{14,10},{7,3},{... | collective-permute-start | bytes 73736 | tf_op jit(solution)/shard_map/ppermute | solution.py:20
  65.7 78.8 %all-reduce.9.cloned.1.call-start = ((), (), s32[]{:S(2)}) async-start(), calls=%async_computation.1 | async-start | bytes 1048576 | tf_op jit(solution)/shard_map/psum | solution.py:111
  65.8 0.7 copy-start.15
  66.5 1.1 copy-start.17
  66.5 1.1 copy-start.22
  66.5 1.1 copy-start.24
  66.5 1.1 copy-start.26
  66.5 1.1 copy-start.28
  66.5 1.1 copy-start.30
  66.5 1.1 copy-start.32
  66.5 1.1 copy-start.34
  144.5 1.7 %copy-start.8 = (f32[2,256,128]{2,1,0:T(8,128)S(1)}, f32[2,256,128]{2,1,0:T(8,128)}, u32[]{:S(2)}) copy-start(f32[2,256,128]{2,1,0:T(8,128)} %get-tuple-element.76) | copy-start | bytes 786436
Sparse Core Ops, SparseCore 0:
  65.8 36.9 all-reduce.6
  105.2 39.2 all-reduce.8
